TPU v7x, 32 devices: a whole 2x2x4 slice. The times are simulated.
32 devices in a mesh: groups: 2 (over y), expert: 16 (over z, x, core).
Axes of the slice: x: 2, y: 2, z: 4, core: 2. Of those that a mesh axis runs over, the one named last changes fastest.
Arguments:
- activations: bfloat16 [2, 512, 2048], P(None, ('groups', 'expert')), parts along dimension 1, may hold values from -6 to 6
- pick_weight: float32 [2, 512, 1], P(None, ('groups', 'expert')), parts along dimension 1, may hold values from 0.2 to 1
- expert_ids: int32 [2, 512, 1], P(None, ('groups', 'expert')), parts along dimension 1, may hold values from 0 to 7, as said below
- replica: int32 [2, 512, 1], P(None, ('groups', 'expert')), parts along dimension 1, may hold values from 0 to 4, as said below
- old_home: int32 [8], replicated, may hold values from 0 to 7, each once
- new_expert: int32 [32], P('groups'), parts along dimension 0, may hold values from 0 to 7, as said below
- gate_panel: bfloat16 [16, 2048, 384], P('expert'), may hold values from -0.125 to 0.125
- up_panel: bfloat16 [16, 2048, 384], P('expert'), may hold values from -0.125 to 0.125
- down_panel: bfloat16 [16, 2048, 384], P('expert'), may hold values from -0.21875 to 0.21875
Outputs:
- layer_output: bfloat16 [2, 512, 2048], P(None, ('groups', 'expert')), parts along dimension 1
- slot_load: int32 [32], P(('groups', 'expert')), parts along dimension 0
There are 2 independent parts, one for each index of `groups`. A program takes and returns all parts, laid end to end along the dimension named above; an argument that names none is the same for every part. Nothing has to cross between parts.
Inputs may be any that keep to these rules, and one draw needn't show every extreme that they name: `new_expert`: every expert is held by 1 or 5 slots. `expert_ids`: the 1 expert that a token names are different. replica[s, t, k] is below the number of slots that new_expert gives to expert_ids[s, t, k]. The picks of the 16 tokens of one device in one batch that land on one slot number at most 2, and in each batch some slot receives exactly 2 from every device.
All inputs are finite; a program needn't handle non-finite values.
Results may differ from a plain program's by a relative error of at most 0.0057.
Values may be sent and summed in bfloat16 or wider, within the bound.
No kernel may reach another device: no remote copies, remote signals or barrier semaphores. Data moves between devices by JAX's collectives and lax.ppermute only.
A program may use at most 128 MiB of HBM per device.

v0:
```python
import jax
import jax.numpy as jnp
from jax import lax
from jax.sharding import PartitionSpec as P

LANES = 128


def slot_rank(new_expert, me):
    positions = jnp.arange(new_expert.shape[0], dtype=jnp.int32)
    mine = jnp.sum(jnp.where(positions == me, new_expert, 0))
    rank = jnp.sum(((new_expert == mine) & (positions < me)).astype(jnp.int32))
    return (mine, rank)


def per_device(
    activations,
    pick_weight,
    expert_ids,
    replica,
    old_home,
    new_expert,
    gate_panel,
    up_panel,
    down_panel,
):
    me = lax.axis_index("expert")
    batches, tokens, width = activations.shape
    top = expert_ids.shape[2]
    rows = batches * tokens
    x = activations.reshape(rows, width)
    picks = jnp.concatenate([expert_ids.reshape(rows, top), replica.reshape(rows, top)], axis=1)
    weights = pick_weight.reshape(rows, top)
    picks_all = lax.all_gather(picks, "expert", axis=0, tiled=True)
    weights_all = lax.all_gather(weights, "expert", axis=0, tiled=True)
    x_all = lax.all_gather(x, "expert", axis=0, tiled=True)
    ids_all = picks_all[:, :top]
    rep_all = picks_all[:, top:]
    mine, rank = slot_rank(new_expert, me)
    load = jnp.sum(((ids_all == mine) & (rep_all == rank)).astype(jnp.int32))
    labels = jnp.arange(old_home.shape[0], dtype=jnp.int32)
    held = jnp.sum(jnp.where(old_home == me // 2, labels, 0))
    scale = jnp.sum(jnp.where(ids_all == held, weights_all, 0.0), axis=1, keepdims=True)
    gate = jnp.dot(x_all, gate_panel[0], preferred_element_type=jnp.float32)
    up = jnp.dot(x_all, up_panel[0], preferred_element_type=jnp.float32)
    hidden = (jax.nn.silu(gate) * up).astype(jnp.bfloat16)
    part = lax.dot_general(
        hidden, down_panel[0], (((1,), (1,)), ((), ())), preferred_element_type=jnp.float32
    )
    part = (part * scale).astype(jnp.bfloat16)
    total = lax.psum_scatter(part, "expert", scatter_dimension=0, tiled=True)
    return (total.reshape(batches, tokens, width), load.reshape(1))


def solution(mesh):
    return jax.shard_map(
        per_device,
        mesh=mesh,
        in_specs=(
            P(None, ("groups", "expert"), None),
            P(None, ("groups", "expert"), None),
            P(None, ("groups", "expert"), None),
            P(None, ("groups", "expert"), None),
            P(),
            P("groups"),
            P("expert", None, None),
            P("expert", None, None),
            P("expert", None, None),
        ),
        out_specs=(P(None, ("groups", "expert"), None), P(("groups", "expert"))),
        check_vma=False,
    )
```

profile of v0, /device:TPU:0, one launch (start us, length us, event | category | flops | bytes accessed | tf_op | source)
XLA Modules:
  0.0 146.4 jit_solution(16085344382893016342)
XLA Ops:
  7.2 0.0 copy-start
  7.2 0.0 all-gather.3.cloned.1.call-start
  7.2 0.7 all-gather.3.cloned.1.call-update
  7.9 0.0 reduce-scatter.2.cloned.1.call-start
  8.0 0.5 broadcast.13
  8.5 1.3 reduce.9
  9.8 0.1 reshape.30
  9.9 0.5 broadcast.14
  10.4 1.3 reduce.11
  11.8 0.1 reshape.25
  11.8 1.3 reduce.10
  13.2 0.1 reshape.26
  13.3 23.1 %all-gather = s32[16,32,2]{1,2,0:T(2,128)S(1)} all-gather(s32[1,32,2]{1,2,0:T(2,128)S(1)} %add_bitcast_fusion), channel_id=1, replica_groups=mesh['groups'=2,'expert'=16] {'expert'}, dimensions={0}, use_global_device_ids=true | all-gather | bytes 4352 | tf_op jit(solution)/shard_map/all_gather | solution.py:34
  36.4 0.1 reshape.34
  36.5 1.2 dynamic-slice
  38.4 0.2 dynamic-update-slice
  38.6 29.9 %all-reduce = f32[512]{0:T(512)S(1)} all-reduce(f32[512]{0:T(512)S(1)} %dynamic-update-slice), channel_id=1, replica_groups=mesh['groups'=2,'expert'=16] {'expert'}, use_global_device_ids=true, to_apply=%add | all-reduce | flops 512 | bytes 4096
  68.5 1.3 fusion.20
  69.8 0.6 compare_select_fusion
  70.5 0.0 copy-start.2
  70.5 0.0 all-gather.3.cloned.1.call-done
  70.5 4.3 %fusion.3 = f32[512,384]{1,0:T(8,128)} fusion(bf16[512,2048]{1,0:T(8,128)(2,1)} %all-gather.3.cloned.1.call-done, bf16[1,2048,384]{2,1,0:T(8,128)(2,1)} %param.15), kind=kOutput, calls=%fused_computation.4 | convolution fusion | flops 805306368 | bytes 4456448 | tf_op jit(solution)/shard_map/dot_general | solution.py:44
  74.8 0.0 copy-done
  74.8 0.0 copy-done.2
  74.8 5.5 %multiply_convert_fusion = bf16[512,2048]{1,0:T(8,128)(2,1)} fusion(f32[512]{0:T(512)S(1)} %bitcast.32, bf16[1,2048,384]{2,1,0:T(8,128)(2,1)S(1)} %copy-done, bf16[512,2048]{1,0:T(8,128)(2,1)} %all-gather.3.cloned.1.call-done, bf16[1,2048,384]{2,1,0:T(8,128)(2,1)S(1)} %copy-done.2, f32[512,384]{1,0:T(8,128)} %fusion.3), kind=kOutput, calls=%fused_computation | convolution fusion | flops 1613889536 | bytes 8128512 | tf_op jit(solution)/shard_map/dot_general | solution.py:47
  80.3 0.0 copy-start.1
  80.3 0.0 reduce-scatter.2.cloned.1.call-update
  80.3 0.6 copy-done.1
  81.0 0.6 fusion.21
  81.6 1.3 fusion.22
  82.9 1.9 %fusion.19 = s32[]{:T(128)} fusion(s32[512,2]{0,1:T(2,128)S(1)} %reshape.34, s32[]{:T(128)} %fusion.22, s32[]{:T(128)} %fusion.21), kind=kLoop, calls=%fused_computation.19 | loop fusion | flops 2559 | bytes 4108 | tf_op jit(solution)/shard_map/reduce_sum | solution.py:40
  84.7 54.9 %reduce-scatter.2.cloned.1.call-done = bf16[32,2048]{1,0:T(8,128)(2,1)} async-done(((bf16[512,2048]{1,0:T(8,128)(2,1)}), bf16[32,2048]{1,0:T(8,128)(2,1)}) %reduce-scatter.2.cloned.1.call-update) | async-done | bytes 131088 | tf_op jit(solution)/shard_map/reduce_scatter | solution.py:51
  (3 shorter events, 0.0 us)
Async XLA Ops:
  7.2 67.7 %copy-start = (bf16[1,2048,384]{2,1,0:T(8,128)(2,1)S(1)}, bf16[1,2048,384]{2,1,0:T(8,128)(2,1)}, u32[]{:S(2)}) copy-start(bf16[1,2048,384]{2,1,0:T(8,128)(2,1)} %param.17) | copy-start | bytes 4718596
  7.2 63.3 %all-gather.3.cloned.1.call-start = ((), (), s32[]{:S(2)}) async-start(), calls=%async_computation.1 | async-start | bytes 2228224 | tf_op jit(solution)/shard_map/all_gather | solution.py:36
  7.9 131.7 %reduce-scatter.2.cloned.1.call-start = ((), (), s32[]{:S(2)}) async-start(), calls=%async_computation.2 | async-start | bytes 2228224 | tf_op jit(solution)/shard_map/reduce_scatter | solution.py:51
  70.5 4.3 %copy-start.2 = (bf16[1,2048,384]{2,1,0:T(8,128)(2,1)S(1)}, bf16[1,2048,384]{2,1,0:T(8,128)(2,1)}, u32[]{:S(2)}) copy-start(bf16[1,2048,384]{2,1,0:T(8,128)(2,1)} %param.16) | copy-start | bytes 4718596
  80.3 0.7 copy-start.1
Sparse Core Ops, SparseCore 0:
  10.1 44.4 all-gather.2
  80.4 59.1 reduce-scatter.1
where the time goes:
time: 147 us; the launch traced here: 146 us
  waiting for transfers between devices  55.6 us (38%)
  blocking collectives  53 us (36%)
  between operations  14.7 us (10%)
  matrix products  9.76 us (7%)
  other arithmetic  9.75 us (7%)
  local copies, waits for them, and re-layouts  3.49 us (2%)
    reduce_scatter x1, waiting for transfers between devices, per_device(): total = lax.psum_scatter(part, 'expert', scatter_dimension=0, tiled=True)  54.9 us
    unnamed x1, blocking collectives  29.9 us
    all_gather x1, blocking collectives, per_device(): picks_all = lax.all_gather(picks, 'expert', axis=0, tiled=True)  23.1 us
    dot_general x1, matrix products, per_device(): lax.dot_general(hidden, down_panel[0], (((1,), (1,)), ((), ())), preferre...  5.48 us
    dot_general x1, matrix products, per_device(): gate = jnp.dot(x_all, gate_panel[0], preferred_element_type=jnp.float32)  4.28 us
    unnamed x4, other arithmetic  4.04 us
    unnamed x13, local copies, waits for them, and re-layouts  3.32 us
  transfers between devices with their start and end apart: 2, of which 1 were waited for; matrix products, arithmetic and copies ran while one was open for 9% of the time, Pallas kernels for 0%

commit v1 on v0

--- a/solution.py
+++ b/solution.py
@@ -31,8 +31,11 @@
     x = activations.reshape(rows, width)
     picks = jnp.concatenate([expert_ids.reshape(rows, top), replica.reshape(rows, top)], axis=1)
     weights = pick_weight.reshape(rows, top)
-    picks_all = lax.all_gather(picks, "expert", axis=0, tiled=True)
-    weights_all = lax.all_gather(weights, "expert", axis=0, tiled=True)
+    picks_all, weights_all = jnp.split(
+        lax.all_gather(jnp.concatenate([picks, weights], axis=1), "expert", axis=0, tiled=True),
+        [picks.shape[1]],
+        axis=1,
+    )
     x_all = lax.all_gather(x, "expert", axis=0, tiled=True)
     ids_all = picks_all[:, :top]
     rep_all = picks_all[:, top:]

time: 147 us -> 132 us (0.90)
  blocking collectives: 53 us -> 23.2 us
  waiting for transfers between devices: 55.6 us -> 72.8 us
  other arithmetic: 9.75 us -> 7.91 us
  local copies, waits for them, and re-layouts: 3.49 us -> 2.01 us
    unnamed x1 -> x0, blocking collectives: 29.9 us -> none
    all_gather x1, waiting for transfers between devices: 0.02 us -> 15.9 us  [per_device(): x_all = lax.all_gather(x, 'expert', axis=0, tiled=True)]
    unnamed x13 -> x9, local copies, waits for them, and re-layouts: 3.32 us -> 1.75 us
  transfers between devices with their start and end apart: 2 -> 2, of which waited for: 1 -> 2; matrix products, arithmetic and copies ran while one was open for 9% -> 7% of each run, Pallas kernels for 0% -> 0%
where the time goes in v1:
time: 132 us
  waiting for transfers between devices  72.8 us (55%)
  blocking collectives  23.2 us (18%)
  between operations  16 us (12%)
  matrix products  9.64 us (7%)
  other arithmetic  7.91 us (6%)
  local copies, waits for them, and re-layouts  2.01 us (2%)
    reduce_scatter x1, waiting for transfers between devices, per_device(): total = lax.psum_scatter(part, 'expert', scatter_dimension=0, tiled=True)  56.2 us
    all_gather x1, blocking collectives, per_device(): lax.all_gather(jnp.concatenate([picks, weights], axis=1), 'expert', axis=...  23.2 us
    all_gather x1, waiting for transfers between devices, per_device(): x_all = lax.all_gather(x, 'expert', axis=0, tiled=True)  15.9 us
    dot_general x1, matrix products, per_device(): lax.dot_general(hidden, down_panel[0], (((1,), (1,)), ((), ())), preferre...  5.47 us
    dot_general x1, matrix products, per_device(): gate = jnp.dot(x_all, gate_panel[0], preferred_element_type=jnp.float32)  4.17 us
    unnamed x4, other arithmetic  4.04 us
  transfers between devices with their start and end apart: 2, of which 2 were waited for; matrix products, arithmetic and copies ran while one was open for 7% of the time, Pallas kernels for 0%

profile of v1, /device:TPU:0, one launch (start us, length us, event | category | flops | bytes accessed | tf_op | source)
XLA Modules:
  0.0 131.7 jit_solution(4512099554793151158)
XLA Ops:
  7.2 0.0 copy-start
  7.2 0.0 all-gather.3.cloned.1.call-start
  7.2 0.7 all-gather.3.cloned.1.call-update
  7.9 0.0 reduce-scatter.2.cloned.1.call-start
  8.0 1.3 fusion.20
  9.9 0.5 broadcast.15
  10.4 1.3 %reduce.9 = f32[2,16]{1,0:T(2,128)S(1)} reduce(f32[2,16,1]{1,2,0:T(1,128)} %param.10, f32[]{:T(128)} %broadcast.15), dimensions={2}, to_apply=%param.10.reduce_sub_computation.3 | reduce | bytes 260 | tf_op args[1]
  11.8 0.1 reshape.27
  11.9 0.5 broadcast.16
  12.4 1.3 %reduce.11 = s32[2,16]{1,0:T(2,128)S(1)} reduce(s32[2,16,1]{1,2,0:T(1,128)} %param.11, s32[]{:T(128)} %broadcast.16), dimensions={2}, to_apply=%param.11.reduce_sub_computation.3 | reduce | bytes 260 | tf_op args[2]
  13.7 0.1 reshape.25
  13.8 1.3 %reduce.10 = s32[2,16]{1,0:T(2,128)S(1)} reduce(s32[2,16,1]{1,2,0:T(1,128)} %param.12, s32[]{:T(128)} %broadcast.16), dimensions={2}, to_apply=%param.12.reduce_sub_computation.3 | reduce | bytes 260 | tf_op args[3]
  15.1 0.1 reshape.26
  15.2 23.2 %all-gather = f32[16,32,3]{1,2,0:T(4,128)S(1)} all-gather(f32[1,32,3]{1,2,0:T(4,128)S(1)} %maximum_bitcast_fusion), channel_id=1, replica_groups=mesh['groups'=2,'expert'=16] {'expert'}, dimensions={0}, use_global_device_ids=true | all-gather | bytes 6528 | tf_op jit(solution)/shard_map/all_gather | solution.py:35
  38.5 0.1 reshape.31
  38.6 0.0 copy-start.2
  38.6 15.9 %all-gather.3.cloned.1.call-done = bf16[512,2048]{1,0:T(8,128)(2,1)} async-done(((bf16[32,2048]{1,0:T(8,128)(2,1)}), bf16[512,2048]{1,0:T(8,128)(2,1)}) %all-gather.3.cloned.1.call-update) | async-done | bytes 2097168 | tf_op jit(solution)/shard_map/all_gather | solution.py:39
  54.5 4.2 %fusion.3 = f32[512,384]{1,0:T(8,128)} fusion(bf16[512,2048]{1,0:T(8,128)(2,1)} %all-gather.3.cloned.1.call-done, bf16[1,2048,384]{2,1,0:T(8,128)(2,1)} %param.15), kind=kOutput, calls=%fused_computation.4 | convolution fusion | flops 805306368 | bytes 4456448 | tf_op jit(solution)/shard_map/dot_general | solution.py:47
  58.6 0.0 copy-done
  58.6 0.0 copy-done.2
  58.6 5.5 %multiply_convert_fusion = bf16[512,2048]{1,0:T(8,128)(2,1)} fusion(f32[512]{0:T(512)S(1)} %bitcast.29, bf16[1,2048,384]{2,1,0:T(8,128)(2,1)S(1)} %copy-done, bf16[512,2048]{1,0:T(8,128)(2,1)} %all-gather.3.cloned.1.call-done, bf16[1,2048,384]{2,1,0:T(8,128)(2,1)S(1)} %copy-done.2, f32[512,384]{1,0:T(8,128)} %fusion.3), kind=kOutput, calls=%fused_computation | convolution fusion | flops 1613889536 | bytes 8128512 | tf_op jit(solution)/shard_map/dot_general | solution.py:50
  64.1 0.0 copy-start.1
  64.1 0.0 reduce-scatter.2.cloned.1.call-update
  64.1 0.6 copy-done.1
  64.8 0.6 fusion.21
  66.1 1.3 fusion.22
  68.0 0.6 fusion.19
  68.6 56.2 %reduce-scatter.2.cloned.1.call-done = bf16[32,2048]{1,0:T(8,128)(2,1)} async-done(((bf16[512,2048]{1,0:T(8,128)(2,1)}), bf16[32,2048]{1,0:T(8,128)(2,1)}) %reduce-scatter.2.cloned.1.call-update) | async-done | bytes 131088 | tf_op jit(solution)/shard_map/reduce_scatter | solution.py:54
  (4 shorter events, 0.0 us)
Async XLA Ops:
  7.2 51.5 %copy-start = (bf16[1,2048,384]{2,1,0:T(8,128)(2,1)S(1)}, bf16[1,2048,384]{2,1,0:T(8,128)(2,1)}, u32[]{:S(2)}) copy-start(bf16[1,2048,384]{2,1,0:T(8,128)(2,1)} %param.17) | copy-start | bytes 4718596
  7.2 47.3 %all-gather.3.cloned.1.call-start = ((), (), s32[]{:S(2)}) async-start(), calls=%async_computation.1 | async-start | bytes 2228224 | tf_op jit(solution)/shard_map/all_gather | solution.py:39
  7.9 116.9 %reduce-scatter.2.cloned.1.call-start = ((), (), s32[]{:S(2)}) async-start(), calls=%async_computation.2 | async-start | bytes 2228224 | tf_op jit(solution)/shard_map/reduce_scatter | solution.py:54
  38.6 20.1 %copy-start.2 = (bf16[1,2048,384]{2,1,0:T(8,128)(2,1)S(1)}, bf16[1,2048,384]{2,1,0:T(8,128)(2,1)}, u32[]{:S(2)}) copy-start(bf16[1,2048,384]{2,1,0:T(8,128)(2,1)} %param.16) | copy-start | bytes 4718596
  64.1 0.7 copy-start.1
Sparse Core Ops, SparseCore 0:
  10.1 44.2 all-gather.2
  64.3 60.5 reduce-scatter.1
